TPU v7x, 128 devices: a whole 4x4x4 slice. The times are simulated.
128 devices in a mesh: dp: 16 (over z, y), mp: 8 (over x, core).
Axes of the slice: x: 4, y: 4, z: 4, core: 2. Of those that a mesh axis runs over, the one named last changes fastest.
Arguments:
- residual: bfloat16 [2048, 4096], P('dp', 'mp'), may hold values from -18 to 18
- queries: bfloat16 [2048, 4096], P('dp', 'mp'), may hold values from -20 to 20
- new_keys: bfloat16 [2048, 1024], P('dp', 'mp'), may hold values from -6 to 6
- new_values: bfloat16 [2048, 1024], P('dp', 'mp'), may hold values from -6 to 6
- cache_keys: bfloat16 [2048, 16, 1024], P('dp', None, 'mp'), may hold values from -6 to 6
- cache_values: bfloat16 [2048, 16, 1024], P('dp', None, 'mp'), may hold values from -6 to 6
- cache_len: int32 [1024], replicated, may hold values from 1 to 128, 16384 in all
- page_order: int32 [2048], replicated, may hold values from 0 to 2047, each once
- out_proj: bfloat16 [4096, 4096], P('mp'), may hold values from -0.09375 to 0.09375
- attn_gain: float32 [4096], replicated, may hold values from 0.25 to 1.75
- routes: int32 [2048, 2], P('dp'), may hold values from 0 to 7, all different within a row; in each aligned block of 128 rows (0 to 127, 128 to 255, ...) at most 48 rows name the same one
- route_weight: float32 [2048, 2], P('dp'), may hold values from 0.1 to 1
- gate_proj: bfloat16 [4096, 98304], P(None, ('dp', 'mp')), may hold values from -0.09375 to 0.09375
- up_proj: bfloat16 [4096, 98304], P(None, ('dp', 'mp')), may hold values from -0.09375 to 0.09375
- down_proj: bfloat16 [98304, 4096], P(('dp', 'mp')), may hold values from -0.0546875 to 0.0546875
- final_gain: float32 [4096], P('mp'), may hold values from 0.25 to 1.75
Outputs:
- layer_out: bfloat16 [2048, 4096], P('dp', 'mp')
Inputs may be any that keep to these rules, and one draw needn't show every extreme that they name: `routes`: in each aligned block of 128 rows (the rows of one dp group) no expert is named by more than 48 rows, a bound that some block reaches; a row's two experts differ. `cache_len`: the lengths sum to 16384, and the longest is exactly 128. `page_order`: each page number appears once; pages past the last request's are unused.
All inputs are finite; a program needn't handle non-finite values.
Results may differ from a plain program's by a relative error of at most 0.008.
Values may be sent and summed in bfloat16 or wider, within the bound.
A program may use at most 128 MiB of HBM per device.

v0:
```python
import jax
import jax.numpy as jnp
from jax import lax
from jax.sharding import PartitionSpec as P

D = 4096
HQ = 32
KVH = 8
HD = 128
E = 8
PAGE = 16
DEC = 64
PRE = 64
C = 48
neg_big = -1e30
eps_norm = 1e-05


def page_owner(page_ids, page_order, cache_len):
    page_count = (cache_len + PAGE - 1) // PAGE
    page_ends = jnp.cumsum(page_count)
    page_first = page_ends - page_count
    pool_iota = lax.broadcasted_iota(jnp.int32, (1, page_order.shape[0]), 1)
    order_pos = jnp.sum(jnp.where(page_order[None, :] == page_ids[:, None], pool_iota, 0), axis=1)
    owners = jnp.sum((page_ends[None, :] <= order_pos[:, None]).astype(jnp.int32), axis=1)
    request_iota = lax.broadcasted_iota(jnp.int32, (1, cache_len.shape[0]), 1)
    chosen = request_iota == owners[:, None]
    first_own = jnp.sum(jnp.where(chosen, page_first[None, :], 0), axis=1)
    length_own = jnp.sum(jnp.where(chosen, cache_len[None, :], 0), axis=1)
    offsets = lax.broadcasted_iota(jnp.int32, (1, PAGE), 1)
    key_pos = (order_pos - first_own)[:, None] * PAGE + offsets
    return (owners, key_pos < length_own[:, None])


def page_partials(page_queries, key_pages, value_pages, key_ok, scale):
    scores = (
        jnp.einsum("pkgh,pokh->pkgo", page_queries, key_pages, preferred_element_type=jnp.float32)
        * scale
    )
    wide_mask = key_ok[:, None, None, :]
    masked = jnp.where(wide_mask, scores, neg_big)
    maxima = jnp.max(masked, axis=3)
    weights = jnp.where(wide_mask, jnp.exp(masked - maxima[..., None]), 0.0)
    totals = jnp.sum(weights, axis=3)
    weighted = jnp.einsum(
        "pkgo,pokh->pkgh",
        weights,
        value_pages.astype(jnp.float32),
        precision=lax.Precision.HIGHEST,
        preferred_element_type=jnp.float32,
    )
    return (maxima, totals, weighted)


def fold_pages(maxima, totals, weighted, owned, local_owner):
    top_score = jnp.max(jnp.where(owned[:, :, None, None], maxima[:, None], neg_big), axis=0)
    page_top = top_score[local_owner]
    factors = jnp.exp(maxima - page_top)
    owned_float = owned.astype(jnp.float32)
    sums = jnp.einsum("pr,pkg->rkg", owned_float, totals * factors, precision=lax.Precision.HIGHEST)
    values = jnp.einsum(
        "pr,pkgh->rkgh", owned_float, weighted * factors[..., None], precision=lax.Precision.HIGHEST
    )
    return (top_score, sums, values)


def local(
    residual,
    queries,
    new_keys,
    new_values,
    cache_keys,
    cache_values,
    cache_len,
    page_order,
    out_proj,
    attn_gain,
    routes,
    route_weight,
    gate_proj,
    up_proj,
    down_proj,
    final_gain,
):
    dp_count = lax.axis_size("dp")
    dp_index = lax.axis_index("dp")
    mp_index = lax.axis_index("mp")
    scale = HD ** (-0.5)
    kv_local = new_keys.shape[1] // HD
    group_size = HQ // KVH
    width_local = residual.shape[1]
    pool_local = cache_keys.shape[0]
    request_total = cache_len.shape[0]
    query_heads = queries[:DEC].reshape(DEC, kv_local, group_size, HD)
    gathered = lax.all_gather(queries[:DEC], "dp", axis=0, tiled=True)
    gathered_heads = gathered.reshape(request_total, kv_local, group_size, HD)
    page_ids = dp_index * pool_local + lax.broadcasted_iota(jnp.int32, (pool_local,), 0)
    owners, key_ok = page_owner(page_ids, page_order, cache_len)
    live = owners < request_total
    local_owner = jnp.minimum(owners, request_total - 1)
    key_ok = key_ok & live[:, None]
    key_pages = cache_keys.reshape(pool_local, PAGE, kv_local, HD)
    value_pages = cache_values.reshape(pool_local, PAGE, kv_local, HD)
    page_queries = gathered_heads[local_owner]
    maxima, totals, weighted = page_partials(page_queries, key_pages, value_pages, key_ok, scale)
    owned = (local_owner[:, None] == lax.broadcasted_iota(jnp.int32, (1, request_total), 1)) & live[
        :, None
    ]
    maxima, totals, weighted = fold_pages(maxima, totals, weighted, owned, local_owner)
    maxima = maxima.reshape(dp_count, DEC, kv_local, group_size)
    totals = totals.reshape(dp_count, DEC, kv_local, group_size)
    weighted = weighted.reshape(dp_count, DEC, kv_local, group_size, HD)
    maxima, totals, weighted = (
        lax.all_to_all(maxima, "dp", split_axis=0, concat_axis=0, tiled=True),
        lax.all_to_all(totals, "dp", split_axis=0, concat_axis=0, tiled=True),
        lax.all_to_all(weighted, "dp", split_axis=0, concat_axis=0, tiled=True),
    )
    top_cache = jnp.max(maxima, axis=0)
    factors = jnp.exp(maxima - top_cache[None])
    cache_state = (
        top_cache,
        jnp.sum(totals * factors, axis=0),
        jnp.sum(weighted * factors[..., None], axis=0),
    )
    self_keys = new_keys[:DEC].reshape(DEC, kv_local, HD)
    self_values = new_values[:DEC].reshape(DEC, kv_local, HD).astype(jnp.float32)
    self_score = (
        jnp.einsum("rkgh,rkh->rkg", query_heads, self_keys, preferred_element_type=jnp.float32)
        * scale
    )
    cache_top, cache_total, cache_sum = cache_state
    top_score = jnp.maximum(cache_top, self_score)
    cache_factor = jnp.exp(cache_top - top_score)
    self_factor = jnp.exp(self_score - top_score)
    numerator = (
        cache_sum * cache_factor[..., None] + self_factor[..., None] * self_values[:, :, None, :]
    )
    denominator = cache_total * cache_factor + self_factor
    decode_out = (numerator / denominator[..., None]).astype(jnp.bfloat16).reshape(DEC, -1)
    prompt_q = queries[DEC:].reshape(PRE, kv_local, group_size, HD)
    prompt_k = new_keys[DEC:].reshape(PRE, kv_local, HD)
    prompt_v = new_values[DEC:].reshape(PRE, kv_local, HD).astype(jnp.float32)
    prompt_scores = (
        jnp.einsum("qkgh,tkh->kgqt", prompt_q, prompt_k, preferred_element_type=jnp.float32) * scale
    )
    causal = lax.broadcasted_iota(jnp.int32, (PRE, PRE), 0) >= lax.broadcasted_iota(
        jnp.int32, (PRE, PRE), 1
    )
    masked = jnp.where(causal, prompt_scores, neg_big)
    top_prompt = jnp.max(masked, axis=-1, keepdims=True)
    prompt_weights = jnp.where(causal, jnp.exp(masked - top_prompt), 0.0)
    prompt_num = jnp.einsum(
        "kgqt,tkh->qkgh",
        prompt_weights,
        prompt_v,
        precision=lax.Precision.HIGHEST,
        preferred_element_type=jnp.float32,
    )
    prompt_den = jnp.sum(prompt_weights, axis=-1).transpose(2, 0, 1)
    prompt_out = (prompt_num / prompt_den[..., None]).astype(jnp.bfloat16).reshape(PRE, -1)
    attn = jnp.concatenate([decode_out, prompt_out], axis=0)
    head_terms = jnp.dot(attn, out_proj, preferred_element_type=jnp.float32)
    column_start = mp_index * width_local
    own_columns = lax.dynamic_slice_in_dim(
        head_terms, column_start, width_local, 1
    ) + residual.astype(jnp.float32)
    head_terms = lax.dynamic_update_slice_in_dim(head_terms, own_columns, column_start, 1)
    hidden_full = lax.psum(head_terms, "mp")
    normed = (
        hidden_full
        * lax.rsqrt(jnp.mean(hidden_full * hidden_full, axis=1, keepdims=True) + eps_norm)
        * attn_gain[None, :]
    ).astype(jnp.bfloat16)
    hidden_cols = lax.dynamic_slice_in_dim(hidden_full, column_start, width_local, 1)
    tok_rows = residual.shape[0]
    pairs = routes.reshape(-1)
    onehot = (pairs[:, None] == lax.broadcasted_iota(jnp.int32, (1, E), 1)).astype(jnp.int32)
    slots = jnp.sum((jnp.cumsum(onehot, axis=0) - onehot) * onehot, axis=1)
    target = pairs * C + slots
    cells = lax.broadcasted_iota(jnp.int32, (1, E * C), 1)
    hits = (target[:, None] == cells).reshape(tok_rows, 2, E * C)
    dispatch = jnp.any(hits, axis=1).astype(jnp.bfloat16)
    combine = jnp.sum(jnp.where(hits, route_weight[:, :, None], 0.0), axis=1)
    buffer = lax.dot_general(
        dispatch, normed, (((0,), (0,)), ((), ())), preferred_element_type=jnp.float32
    ).astype(jnp.bfloat16)
    send = jnp.repeat(buffer.reshape(E, C, normed.shape[1]), dp_count // E, axis=0)
    arrived = lax.all_to_all(send, "dp", split_axis=0, concat_axis=0, tiled=True)
    gate_sum = jnp.einsum("scd,df->scf", arrived, gate_proj, preferred_element_type=jnp.float32)
    up_sum = jnp.einsum("scd,df->scf", arrived, up_proj, preferred_element_type=jnp.float32)
    hidden = (jax.nn.silu(gate_sum) * up_sum).astype(jnp.bfloat16)
    down_part = jnp.einsum("scf,fd->scd", hidden, down_proj, preferred_element_type=jnp.float32)
    shares = lax.psum_scatter(
        down_part.astype(jnp.bfloat16), "mp", scatter_dimension=2, tiled=True
    ).astype(jnp.float32)
    returned = lax.all_to_all(shares, "dp", split_axis=0, concat_axis=0, tiled=True)
    back = (
        returned.reshape(E, dp_count // E, C, width_local).sum(axis=1).reshape(E * C, width_local)
    )
    moe_rows = jnp.dot(
        combine, back, precision=lax.Precision.HIGHEST, preferred_element_type=jnp.float32
    )
    mixed = hidden_cols + moe_rows
    square_last = lax.psum(jnp.sum(mixed * mixed, axis=1), "mp")
    scaled = mixed * lax.rsqrt(square_last / D + eps_norm)[:, None] * final_gain[None, :]
    return scaled.astype(jnp.bfloat16)


def solution(mesh):
    return jax.shard_map(
        local,
        mesh=mesh,
        in_specs=(
            P("dp", "mp"),
            P("dp", "mp"),
            P("dp", "mp"),
            P("dp", "mp"),
            P("dp", None, "mp"),
            P("dp", None, "mp"),
            P(),
            P(),
            P("mp", None),
            P(),
            P("dp", None),
            P("dp", None),
            P(None, ("dp", "mp")),
            P(None, ("dp", "mp")),
            P(("dp", "mp"), None),
            P("mp"),
        ),
        out_specs=P("dp", "mp"),
        check_vma=False,
    )
```

profile of v0, /device:TPU:0, one launch (start us, length us, event | category | flops | bytes accessed | tf_op | source)
XLA Modules:
  0.0 386.7 jit_solution(8558500685093032469)
XLA Ops:
  6.5 1.6 fusion.67
  8.2 0.7 fusion.64
  8.9 0.3 reduce-window.15
  9.4 0.8 fusion.63
  10.1 1.0 select_reduce_fusion.1
  11.3 0.9 select_reduce_fusion.3
  12.6 42.3 %all-gather.2.cloned.1.call-done = bf16[1024,512]{1,0:T(8,128)(2,1)} async-done(((bf16[64,512]{1,0:T(8,128)(2,1)}), bf16[1024,512]{1,0:T(8,128)(2,1)}) %all-gather.2.cloned.1.call-update) | async-done | bytes 1048592 | tf_op jit(solution)/shard_map/all_gather | solution.py:95
  54.9 1.3 reshape.430
  56.2 0.7 gather_fusion
  57.0 0.5 fusion.69
  57.5 0.3 select_reduce_fusion
  58.1 0.7 gather_fusion.1
  58.7 0.4 fusion.25
  59.1 0.8 fusion.70
  59.9 0.7 reshape.468
  60.6 4.9 %all-to-all-start.2 = ((f32[16,1,256]{2,1,0:T(1,128)}), f32[16,1,256]{2,1,0:T(1,128)S(1)}, u32[]{:S(2)}, u32[]{:S(2)}) async-start(f32[16,1,256]{2,1,0:T(1,128)} %reshape.468), calls=%async_computation.2 | async-start | bytes 32768 | tf_op jit(solution)/shard_map/all_to_all | solution.py:115
  65.6 0.7 fusion.7
  66.5 0.7 reshape.466
  67.2 5.9 %all-to-all-done.2 = f32[16,1,256]{2,1,0:T(1,128)S(1)} async-done(((f32[16,1,256]{2,1,0:T(1,128)}), f32[16,1,256]{2,1,0:T(1,128)S(1)}, u32[]{:S(2)}, u32[]{:S(2)}) %all-to-all-start.2) | async-done | bytes 16416 | tf_op jit(solution)/shard_map/all_to_all | solution.py:115
  73.1 3.5 all-to-all-start.1
  76.6 2.4 convolution_bitcast_fusion
  79.0 5.1 %all-to-all-done.1 = f32[16,1,256]{2,1,0:T(1,128)S(1)} async-done(((f32[16,1,256]{2,1,0:T(1,128)}), f32[16,1,256]{2,1,0:T(1,128)S(1)}, u32[]{:S(2)}, u32[]{:S(2)}) %all-to-all-start.1) | async-done | bytes 16416 | tf_op jit(solution)/shard_map/all_to_all | solution.py:114
  84.2 3.7 all-to-all-start
  88.6 0.3 fusion.12
  89.0 0.5 broadcast.295
  89.5 0.7 reduce.15
  90.3 0.7 reduce.14
  91.1 24.1 %all-to-all-done = f32[16,64,1,4,128]{4,1,3,2,0:T(8,128)S(1)} async-done(((f32[16,64,1,4,128]{4,1,3,2,0:T(8,128)}), f32[16,64,1,4,128]{4,1,3,2,0:T(8,128)S(1)}, u32[]{:S(2)}, u32[]{:S(2)}) %all-to-all-start) | async-done | bytes 2097184 | tf_op jit(solution)/shard_map/all_to_all | solution.py:116
  115.2 0.7 bitcast_reduce_fusion
  116.1 2.9 fusion.26
  119.1 1.3 copy-done.2
  120.9 0.6 reduce-window.19
  122.2 60.5 %all-reduce.2.cloned.1.call-done = f32[128,4096]{1,0:T(8,128)} async-done(((f32[128,4096]{1,0:T(8,128)}), f32[128,4096]{1,0:T(8,128)}) %all-reduce.2.cloned.1.call-update) | async-done | bytes 2097168 | tf_op jit(solution)/shard_map/psum | solution.py:168
  182.7 2.0 multiply_reduce_fusion
  185.0 1.1 convolution_convert_fusion.1
  186.0 0.8 broadcast_in_dim.146
  186.8 79.0 %all_to_all.25 = bf16[16,48,4096]{2,1,0:T(8,128)(2,1)S(1)} all-to-all(bf16[16,48,4096]{2,1,0:T(8,128)(2,1)S(1)} %bitcast.149), channel_id=1, replica_groups=mesh['dp'=16,'mp'=8] {'dp'}, dimensions={0} | all-to-all | bytes 12582912 | tf_op jit(solution)/shard_map/all_to_all | solution.py:188
  265.8 7.5 %fusion.1 = f32[16,48,768]{2,1,0:T(8,128)S(1)} fusion(bf16[16,48,4096]{2,1,0:T(8,128)(2,1)S(1)} %all_to_all.25, bf16[4096,768]{1,0:T(8,128)(2,1)} %param.29), kind=kOutput, calls=%fused_computation.4 | convolution fusion | flops 4831838208 | bytes 14942208 | tf_op jit(solution)/shard_map/scd,df->scf/dot_general | solution.py:190
  273.3 5.3 %multiply_convert_fusion = bf16[16,48,768]{2,1,0:T(8,128)(2,1)S(1)} fusion(f32[16,48,768]{2,1,0:T(8,128)S(1)} %fusion.1, bf16[16,48,4096]{2,1,0:T(8,128)(2,1)S(1)} %all_to_all.25, bf16[4096,768]{1,0:T(8,128)(2,1)S(1)} %bitcast.157), kind=kOutput, calls=%fused_computation.9 | convolution fusion | flops 4835377152 | bytes 16121856 | tf_op jit(solution)/shard_map/scd,df->scf/dot_general | solution.py:189
  278.7 6.9 %convolution_convert_fusion = bf16[16,48,4096]{2,1,0:T(8,128)(2,1)} fusion(bf16[16,48,768]{2,1,0:T(8,128)(2,1)S(1)} %multiply_convert_fusion, bf16[768,4096]{1,0:T(8,128)(2,1)S(1)} %bitcast.159), kind=kOutput, calls=%fused_computation.2 | convolution fusion | flops 4834983936 | bytes 13762560 | tf_op jit(solution)/shard_map/scf,fd->scd/dot_general | solution.py:192
  285.6 41.4 %reduce-scatter.2.cloned.1.call-done = bf16[16,48,512]{2,1,0:T(8,128)(2,1)} async-done(((bf16[16,48,4096]{2,1,0:T(8,128)(2,1)}), bf16[16,48,512]{2,1,0:T(8,128)(2,1)}) %reduce-scatter.2.cloned.1.call-update) | async-done | bytes 786448 | tf_op jit(solution)/shard_map/reduce_scatter | solution.py:193
  327.0 2.5 convert_element_type.63
  329.5 7.0 %all-to-all-start.4 = ((f32[16,48,512]{2,1,0:T(8,128)}), f32[16,48,512]{2,1,0:T(8,128)}, u32[]{:S(2)}, u32[]{:S(2)}) async-start(f32[16,48,512]{2,1,0:T(8,128)} %convert_element_type.63), calls=%async_computation.5 | async-start | bytes 3145728 | tf_op jit(solution)/shard_map/all_to_all | solution.py:196
  336.7 23.3 %all-to-all-done.4 = f32[16,48,512]{2,1,0:T(8,128)} async-done(((f32[16,48,512]{2,1,0:T(8,128)}), f32[16,48,512]{2,1,0:T(8,128)}, u32[]{:S(2)}, u32[]{:S(2)}) %all-to-all-start.4) | async-done | bytes 1572896 | tf_op jit(solution)/shard_map/all_to_all | solution.py:196
  360.1 1.6 bitcast_reduce_fusion.1
  361.7 0.7 multiply_reduce_fusion.1
  362.4 17.0 %psum.15 = f32[128]{0:T(128)S(1)} all-reduce(f32[128]{0:T(128)S(1)} %get-tuple-element.20), channel_id=1, replica_groups=mesh['dp'=16,'mp'=8] {'mp'}, use_global_device_ids=true, to_apply=%region_24.25 | all-reduce | flops 128 | bytes 1024 | tf_op jit(solution)/shard_map/psum | solution.py:204
  379.4 0.8 multiply_convert_fusion.3
  (93 shorter events, 4.1 us)
Async XLA Ops:
  6.5 59.0 %copy-start = (bf16[128,16,128]{2,1,0:T(8,128)(2,1)S(1)}, bf16[128,16,128]{2,1,0:T(8,128)(2,1)}, u32[]{:S(2)}) copy-start(bf16[128,16,128]{2,1,0:T(8,128)(2,1)} %param.21) | copy-start | bytes 1572868
  6.5 50.5 %copy-start.5 = (bf16[128,16,128]{2,1,0:T(8,128)(2,1)S(1)}, bf16[128,16,128]{2,1,0:T(8,128)(2,1)}, u32[]{:S(2)}) copy-start(bf16[128,16,128]{2,1,0:T(8,128)(2,1)} %param.20) | copy-start | bytes 1572868
  6.5 48.4 %all-gather.2.cloned.1.call-start = ((), (), s32[]{:S(2)}) async-start(), calls=%async_computation.6 | async-start | bytes 1114112 | tf_op jit(solution)/shard_map/all_gather | solution.py:95
  60.6 12.5 %all-to-all-start.2 = ((f32[16,1,256]{2,1,0:T(1,128)}), f32[16,1,256]{2,1,0:T(1,128)S(1)}, u32[]{:S(2)}, u32[]{:S(2)}) async-start(f32[16,1,256]{2,1,0:T(1,128)} %reshape.468), calls=%async_computation.2 | async-start | bytes 32768 | tf_op jit(solution)/shard_map/all_to_all | solution.py:115
  73.1 11.0 %all-to-all-start.1 = ((f32[16,1,256]{2,1,0:T(1,128)}), f32[16,1,256]{2,1,0:T(1,128)S(1)}, u32[]{:S(2)}, u32[]{:S(2)}) async-start(f32[16,1,256]{2,1,0:T(1,128)} %reshape.466), calls=%async_computation.1 | async-start | bytes 32768 | tf_op jit(solution)/shard_map/all_to_all | solution.py:114
  79.0 8.9 %copy-start.4 = (bf16[64,512]{1,0:T(8,128)(2,1)S(1)}, bf16[64,512]{1,0:T(8,128)(2,1)}, u32[]{:S(2)}) copy-start(bf16[64,512]{1,0:T(8,128)(2,1)} %get-tuple-element.12) | copy-start | bytes 196612
  79.0 9.0 %copy-start.7 = (bf16[128,128]{1,0:T(8,128)(2,1)S(1)}, bf16[128,128]{1,0:T(8,128)(2,1)}, u32[]{:S(2)}) copy-start(bf16[128,128]{1,0:T(8,128)(2,1)} %param.18) | copy-start | bytes 98308
  79.0 9.5 %copy-start.9 = (bf16[128,128]{1,0:T(8,128)(2,1)S(1)}, bf16[128,128]{1,0:T(8,128)(2,1)}, u32[]{:S(2)}) copy-start(bf16[128,128]{1,0:T(8,128)(2,1)} %param.19) | copy-start | bytes 98308
  84.2 31.0 %all-to-all-start = ((f32[16,64,1,4,128]{4,1,3,2,0:T(8,128)}), f32[16,64,1,4,128]{4,1,3,2,0:T(8,128)S(1)}, u32[]{:S(2)}, u32[]{:S(2)}) async-start(f32[16,64,1,4,128]{4,1,3,2,0:T(8,128)} %convolution_bitcast_fusion), calls=%async_computation | async-start | bytes 4194304 | tf_op jit(solution)/shard_map/all_to_all | solution.py:116
  87.9 94.8 %all-reduce.2.cloned.1.call-start = ((), (), s32[]{:S(2)}) async-start(), calls=%async_computation.7 | async-start | bytes 4194304 | tf_op jit(solution)/shard_map/psum | solution.py:168
  116.1 3.0 copy-start.6
  119.0 1.4 copy-start.10
  119.1 1.3 copy-start.2
  119.1 65.6 %copy-start.8 = (f32[4096]{0:T(1024)S(1)}, f32[4096]{0:T(1024)}, u32[]{:S(2)}) copy-start(f32[4096]{0:T(1024)} %param.25) | copy-start | bytes 49156
  120.4 206.6 %reduce-scatter.2.cloned.1.call-start = ((), (), s32[]{:S(2)}) async-start(), calls=%async_computation.8 | async-start | bytes 7077888 | tf_op jit(solution)/shard_map/reduce_scatter | solution.py:193
  182.7 2.2 copy-start.3
  186.8 86.5 %slice-start = ((s8[6291456]{0:T(1024)(128)(4,1)}), s8[4194304]{0:T(1024)(128)(4,1)S(1)}, s32[]{:S(2)}) async-start(s8[6291456]{0:T(1024)(128)(4,1)} %bitcast.156), calls=%async_computation.9 | async-start | bytes 8388608
  265.8 7.5 %slice-start.1 = ((s8[6291456]{0:T(1024)(128)(4,1)}), s8[2097152]{0:T(1024)(128)(4,1)S(1)}, s32[]{:S(2)}) async-start(s8[6291456]{0:T(1024)(128)(4,1)} %bitcast.156), calls=%async_computation.10 | async-start | bytes 4194304
  265.8 12.8 %slice-start.2 = ((s8[6291456]{0:T(1024)(128)(4,1)}), s8[4194304]{0:T(1024)(128)(4,1)S(1)}, s32[]{:S(2)}) async-start(s8[6291456]{0:T(1024)(128)(4,1)} %bitcast.158), calls=%async_computation.11 | async-start | bytes 8388608
  273.3 5.3 %slice-start.3 = ((s8[6291456]{0:T(1024)(128)(4,1)}), s8[2097152]{0:T(1024)(128)(4,1)S(1)}, s32[]{:S(2)}) async-start(s8[6291456]{0:T(1024)(128)(4,1)} %bitcast.158), calls=%async_computation.12 | async-start | bytes 4194304
  285.6 51.0 %copy-start.12 = (f32[128,2]{0,1:T(2,128)S(1)}, f32[128,2]{0,1:T(2,128)}, u32[]{:S(2)}) copy-start(f32[128,2]{0,1:T(2,128)} %param.27) | copy-start | bytes 3076
  329.5 30.5 %all-to-all-start.4 = ((f32[16,48,512]{2,1,0:T(8,128)}), f32[16,48,512]{2,1,0:T(8,128)}, u32[]{:S(2)}, u32[]{:S(2)}) async-start(f32[16,48,512]{2,1,0:T(8,128)} %convert_element_type.63), calls=%async_computation.5 | async-start | bytes 3145728 | tf_op jit(solution)/shard_map/all_to_all | solution.py:196
  336.6 42.8 %copy-start.11 = (f32[512]{0:T(512)S(1)}, f32[512]{0:T(512)}, u32[]{:S(2)}) copy-start(f32[512]{0:T(512)} %param.31) | copy-start | bytes 6148
  336.6 43.6 %copy-start.1 = (bf16[128,16,128]{2,1,0:T(8,128)(2,1)S(1)}, bf16[128,16,128]{2,1,0:T(8,128)(2,1)}, u32[]{:S(2)}) copy-start(bf16[128,16,128]{2,1,0:T(8,128)(2,1)} %param.21) | copy-start | bytes 1572868
Sparse Core Ops, SparseCore 0:
  9.5 45.3 all-gather.1
  120.5 62.1 all-reduce.1
  285.7 41.2 reduce-scatter.1
where the time goes:
time: 387 us
  waiting for transfers between devices  203 us (52%)
  blocking collectives  96 us (25%)
  matrix products  29.4 us (8%)
  starting transfers between devices  19.3 us (5%)
  other arithmetic  15.1 us (4%)
  between operations  13.6 us (4%)
  local copies, waits for them, and re-layouts  10.6 us (3%)
    all_to_all x1, blocking collectives, local(): lax.all_to_all(send, 'dp', split_axis=0, concat_axis=0, tiled=True)  79 us
    psum x1, waiting for transfers between devices, local(): hidden_full = lax.psum(head_terms, 'mp')  60.5 us
    all_gather x1, waiting for transfers between devices, local(): gathered = lax.all_gather(queries[:DEC], 'dp', axis=0, tiled=True)  42.3 us
    reduce_scatter x1, waiting for transfers between devices, local(): lax.psum_scatter(down_part.astype(jnp.bfloat16), 'mp', scatter_dimension=...  41.4 us
    all_to_all x1, waiting for transfers between devices, local(): lax.all_to_all(weighted, 'dp', split_axis=0, concat_axis=0, tiled=True)  24.1 us
    all_to_all x1, waiting for transfers between devices, local(): lax.all_to_all(shares, 'dp', split_axis=0, concat_axis=0, tiled=True)  23.3 us
    psum x1, blocking collectives, local(): square_last = lax.psum(jnp.sum(mixed * mixed, axis=1), 'mp')  17 us
  transfers between devices with their start and end apart: 7, of which 7 were waited for; matrix products, arithmetic and copies ran while one was open for 3% of the time, Pallas kernels for 0%

commit v1 on v0

--- a/solution.py
+++ b/solution.py
@@ -165,7 +165,7 @@
         head_terms, column_start, width_local, 1
     ) + residual.astype(jnp.float32)
     head_terms = lax.dynamic_update_slice_in_dim(head_terms, own_columns, column_start, 1)
-    hidden_full = lax.psum(head_terms, "mp")
+    hidden_full = jnp.sum(lax.all_gather(head_terms, "mp"), axis=0)
     normed = (
         hidden_full
         * lax.rsqrt(jnp.mean(hidden_full * hidden_full, axis=1, keepdims=True) + eps_norm)

time: 387 us -> 413 us (1.067)
  waiting for transfers between devices: 203 us -> 220 us
  other arithmetic: 15.1 us -> 20.7 us
    all_gather x0 -> x1, waiting for transfers between devices: none -> 79.8 us  [local(): hidden_full = jnp.sum(lax.all_gather(head_terms, 'mp'), axis=0)]
    psum x1 -> x0, waiting for transfers between devices: 60.5 us -> none  [local(): hidden_full = lax.psum(head_terms, 'mp')]
    reduce_sum x0 -> x1, other arithmetic: none -> 7.36 us  [local(): hidden_full = jnp.sum(lax.all_gather(head_terms, 'mp'), axis=0)]
where the time goes in v1:
time: 413 us; the launch traced here: 412 us
  waiting for transfers between devices  220 us (53%)
  blocking collectives  97.8 us (24%)
  matrix products  29.4 us (7%)
  other arithmetic  20.7 us (5%)
  starting transfers between devices  19.2 us (5%)
  between operations  13.6 us (3%)
  local copies, waits for them, and re-layouts  11.3 us (3%)
    all_to_all x1, blocking collectives, local(): lax.all_to_all(send, 'dp', split_axis=0, concat_axis=0, tiled=True)  80.8 us
    all_gather x1, waiting for transfers between devices, local(): hidden_full = jnp.sum(lax.all_gather(head_terms, 'mp'), axis=0)  79.8 us
    all_gather x1, waiting for transfers between devices, local(): gathered = lax.all_gather(queries[:DEC], 'dp', axis=0, tiled=True)  42.3 us
    reduce_scatter x1, waiting for transfers between devices, local(): lax.psum_scatter(down_part.astype(jnp.bfloat16), 'mp', scatter_dimension=...  39.3 us
    all_to_all x1, waiting for transfers between devices, local(): lax.all_to_all(weighted, 'dp', split_axis=0, concat_axis=0, tiled=True)  24.1 us
    all_to_all x1, waiting for transfers between devices, local(): lax.all_to_all(shares, 'dp', split_axis=0, concat_axis=0, tiled=True)  23.3 us
    psum x1, blocking collectives, local(): square_last = lax.psum(jnp.sum(mixed * mixed, axis=1), 'mp')  17 us
  transfers between devices with their start and end apart: 7, of which 7 were waited for; matrix products, arithmetic and copies ran while one was open for 3% of the time, Pallas kernels for 0%

profile of v1, /device:TPU:0, one launch (start us, length us, event | category | flops | bytes accessed | tf_op | source)
XLA Modules:
  0.0 411.8 jit_solution(2624498678209332277)
XLA Ops:
  6.5 1.6 fusion.67
  8.2 0.7 fusion.64
  9.4 0.8 fusion.63
  10.1 1.0 select_reduce_fusion.1
  11.3 0.9 select_reduce_fusion.3
  12.6 42.3 %all-gather.3.cloned.1.call-done = bf16[1024,512]{1,0:T(8,128)(2,1)} async-done(((bf16[64,512]{1,0:T(8,128)(2,1)}), bf16[1024,512]{1,0:T(8,128)(2,1)}) %all-gather.3.cloned.1.call-update) | async-done | bytes 1048592 | tf_op jit(solution)/shard_map/all_gather | solution.py:95
  54.9 1.3 reshape.432
  56.2 0.7 gather_fusion
  57.0 0.5 fusion.69
  57.5 0.3 select_reduce_fusion
  58.1 0.7 gather_fusion.1
  58.7 0.4 fusion.25
  59.1 0.8 fusion.70
  59.9 0.7 reshape.470
  60.6 4.9 %all-to-all-start.2 = ((f32[16,1,256]{2,1,0:T(1,128)}), f32[16,1,256]{2,1,0:T(1,128)S(1)}, u32[]{:S(2)}, u32[]{:S(2)}) async-start(f32[16,1,256]{2,1,0:T(1,128)} %reshape.470), calls=%async_computation.2 | async-start | bytes 32768 | tf_op jit(solution)/shard_map/all_to_all | solution.py:115
  65.6 0.7 fusion.7
  66.5 0.7 reshape.468
  67.2 5.9 %all-to-all-done.2 = f32[16,1,256]{2,1,0:T(1,128)S(1)} async-done(((f32[16,1,256]{2,1,0:T(1,128)}), f32[16,1,256]{2,1,0:T(1,128)S(1)}, u32[]{:S(2)}, u32[]{:S(2)}) %all-to-all-start.2) | async-done | bytes 16416 | tf_op jit(solution)/shard_map/all_to_all | solution.py:115
  73.1 3.5 all-to-all-start.1
  76.6 2.4 convolution_bitcast_fusion
  79.0 5.1 %all-to-all-done.1 = f32[16,1,256]{2,1,0:T(1,128)S(1)} async-done(((f32[16,1,256]{2,1,0:T(1,128)}), f32[16,1,256]{2,1,0:T(1,128)S(1)}, u32[]{:S(2)}, u32[]{:S(2)}) %all-to-all-start.1) | async-done | bytes 16416 | tf_op jit(solution)/shard_map/all_to_all | solution.py:114
  84.2 3.7 all-to-all-start
  88.6 0.3 fusion.12
  89.0 0.5 broadcast.295
  89.5 0.7 reduce.15
  90.3 0.7 reduce.14
  91.1 24.1 %all-to-all-done = f32[16,64,1,4,128]{4,1,3,2,0:T(8,128)S(1)} async-done(((f32[16,64,1,4,128]{4,1,3,2,0:T(8,128)}), f32[16,64,1,4,128]{4,1,3,2,0:T(8,128)S(1)}, u32[]{:S(2)}, u32[]{:S(2)}) %all-to-all-start) | async-done | bytes 2097184 | tf_op jit(solution)/shard_map/all_to_all | solution.py:116
  115.2 0.7 bitcast_reduce_fusion
  116.1 2.9 fusion.26
  119.2 0.7 copy-done.5
  119.9 1.3 copy-done.2
  121.8 0.6 reduce-window.19
  123.1 79.8 %all-gather.5.cloned.1.call-done = f32[8,128,4096]{2,1,0:T(8,128)} async-done(((f32[1,128,4096]{2,1,0:T(8,128)}), f32[8,128,4096]{2,1,0:T(8,128)}) %all-gather.5.cloned.1.call-update) | async-done | bytes 16777232 | tf_op jit(solution)/shard_map/all_gather | solution.py:168
  202.9 7.4 %reduce_sum.139 = f32[128,4096]{1,0:T(8,128)S(1)} reduce(f32[8,128,4096]{2,1,0:T(8,128)} %all-gather.5.cloned.1.call-done, f32[]{:T(128)} %constant.69.clone.1), dimensions={0}, to_apply=%region_14.15 | reduce | flops 3670016 | bytes 18874372 | tf_op jit(solution)/shard_map/reduce_sum | solution.py:168
  210.5 1.1 convolution_convert_fusion.1
  211.5 0.8 broadcast_in_dim.146
  212.3 80.8 %all_to_all.25 = bf16[16,48,4096]{2,1,0:T(8,128)(2,1)S(1)} all-to-all(bf16[16,48,4096]{2,1,0:T(8,128)(2,1)S(1)} %bitcast.152), channel_id=1, replica_groups=mesh['dp'=16,'mp'=8] {'dp'}, dimensions={0} | all-to-all | bytes 12582912 | tf_op jit(solution)/shard_map/all_to_all | solution.py:188
  293.1 7.5 %fusion.1 = f32[16,48,768]{2,1,0:T(8,128)S(1)} fusion(bf16[16,48,4096]{2,1,0:T(8,128)(2,1)S(1)} %all_to_all.25, bf16[4096,768]{1,0:T(8,128)(2,1)} %param.29), kind=kOutput, calls=%fused_computation.4 | convolution fusion | flops 4831838208 | bytes 14942208 | tf_op jit(solution)/shard_map/scd,df->scf/dot_general | solution.py:190
  300.6 5.3 %multiply_convert_fusion = bf16[16,48,768]{2,1,0:T(8,128)(2,1)S(1)} fusion(f32[16,48,768]{2,1,0:T(8,128)S(1)} %fusion.1, bf16[16,48,4096]{2,1,0:T(8,128)(2,1)S(1)} %all_to_all.25, bf16[4096,768]{1,0:T(8,128)(2,1)S(1)} %bitcast.161), kind=kOutput, calls=%fused_computation.9 | convolution fusion | flops 4835377152 | bytes 16121856 | tf_op jit(solution)/shard_map/scd,df->scf/dot_general | solution.py:189
  306.0 6.9 %convolution_convert_fusion = bf16[16,48,4096]{2,1,0:T(8,128)(2,1)} fusion(bf16[16,48,768]{2,1,0:T(8,128)(2,1)S(1)} %multiply_convert_fusion, bf16[768,4096]{1,0:T(8,128)(2,1)S(1)} %bitcast.163), kind=kOutput, calls=%fused_computation.2 | convolution fusion | flops 4834983936 | bytes 13762560 | tf_op jit(solution)/shard_map/scf,fd->scd/dot_general | solution.py:192
  312.9 39.3 %reduce-scatter.2.cloned.1.call-done = bf16[16,48,512]{2,1,0:T(8,128)(2,1)} async-done(((bf16[16,48,4096]{2,1,0:T(8,128)(2,1)}), bf16[16,48,512]{2,1,0:T(8,128)(2,1)}) %reduce-scatter.2.cloned.1.call-update) | async-done | bytes 786448 | tf_op jit(solution)/shard_map/reduce_scatter | solution.py:193
  352.2 2.5 convert_element_type.63
  354.7 7.0 %all-to-all-start.4 = ((f32[16,48,512]{2,1,0:T(8,128)}), f32[16,48,512]{2,1,0:T(8,128)}, u32[]{:S(2)}, u32[]{:S(2)}) async-start(f32[16,48,512]{2,1,0:T(8,128)} %convert_element_type.63), calls=%async_computation.5 | async-start | bytes 3145728 | tf_op jit(solution)/shard_map/all_to_all | solution.py:196
  361.9 23.3 %all-to-all-done.4 = f32[16,48,512]{2,1,0:T(8,128)} async-done(((f32[16,48,512]{2,1,0:T(8,128)}), f32[16,48,512]{2,1,0:T(8,128)}, u32[]{:S(2)}, u32[]{:S(2)}) %all-to-all-start.4) | async-done | bytes 1572896 | tf_op jit(solution)/shard_map/all_to_all | solution.py:196
  385.2 1.6 bitcast_reduce_fusion.1
  386.8 0.7 multiply_reduce_fusion.1
  387.6 17.0 %psum.7 = f32[128]{0:T(128)S(1)} all-reduce(f32[128]{0:T(128)S(1)} %get-tuple-element.20), channel_id=1, replica_groups=mesh['dp'=16,'mp'=8] {'mp'}, use_global_device_ids=true, to_apply=%region_24.25 | all-reduce | flops 128 | bytes 1024 | tf_op jit(solution)/shard_map/psum | solution.py:204
  404.5 0.8 multiply_convert_fusion.3
  (93 shorter events, 4.5 us)
Async XLA Ops:
  6.5 59.0 %copy-start = (bf16[128,16,128]{2,1,0:T(8,128)(2,1)S(1)}, bf16[128,16,128]{2,1,0:T(8,128)(2,1)}, u32[]{:S(2)}) copy-start(bf16[128,16,128]{2,1,0:T(8,128)(2,1)} %param.21) | copy-start | bytes 1572868
  6.5 50.5 %copy-start.4 = (bf16[128,16,128]{2,1,0:T(8,128)(2,1)S(1)}, bf16[128,16,128]{2,1,0:T(8,128)(2,1)}, u32[]{:S(2)}) copy-start(bf16[128,16,128]{2,1,0:T(8,128)(2,1)} %param.20) | copy-start | bytes 1572868
  6.5 48.4 %all-gather.3.cloned.1.call-start = ((), (), s32[]{:S(2)}) async-start(), calls=%async_computation.6 | async-start | bytes 1114112 | tf_op jit(solution)/shard_map/all_gather | solution.py:95
  60.6 12.5 %all-to-all-start.2 = ((f32[16,1,256]{2,1,0:T(1,128)}), f32[16,1,256]{2,1,0:T(1,128)S(1)}, u32[]{:S(2)}, u32[]{:S(2)}) async-start(f32[16,1,256]{2,1,0:T(1,128)} %reshape.470), calls=%async_computation.2 | async-start | bytes 32768 | tf_op jit(solution)/shard_map/all_to_all | solution.py:115
  73.1 11.0 %all-to-all-start.1 = ((f32[16,1,256]{2,1,0:T(1,128)}), f32[16,1,256]{2,1,0:T(1,128)S(1)}, u32[]{:S(2)}, u32[]{:S(2)}) async-start(f32[16,1,256]{2,1,0:T(1,128)} %reshape.468), calls=%async_computation.1 | async-start | bytes 32768 | tf_op jit(solution)/shard_map/all_to_all | solution.py:114
  79.0 8.9 %copy-start.3 = (bf16[64,512]{1,0:T(8,128)(2,1)S(1)}, bf16[64,512]{1,0:T(8,128)(2,1)}, u32[]{:S(2)}) copy-start(bf16[64,512]{1,0:T(8,128)(2,1)} %get-tuple-element.12) | copy-start | bytes 196612
  79.0 9.0 %copy-start.6 = (bf16[128,128]{1,0:T(8,128)(2,1)S(1)}, bf16[128,128]{1,0:T(8,128)(2,1)}, u32[]{:S(2)}) copy-start(bf16[128,128]{1,0:T(8,128)(2,1)} %param.18) | copy-start | bytes 98308
  79.0 9.5 %copy-start.8 = (bf16[128,128]{1,0:T(8,128)(2,1)S(1)}, bf16[128,128]{1,0:T(8,128)(2,1)}, u32[]{:S(2)}) copy-start(bf16[128,128]{1,0:T(8,128)(2,1)} %param.19) | copy-start | bytes 98308
  84.2 31.0 %all-to-all-start = ((f32[16,64,1,4,128]{4,1,3,2,0:T(8,128)}), f32[16,64,1,4,128]{4,1,3,2,0:T(8,128)S(1)}, u32[]{:S(2)}, u32[]{:S(2)}) async-start(f32[16,64,1,4,128]{4,1,3,2,0:T(8,128)} %convolution_bitcast_fusion), calls=%async_computation | async-start | bytes 4194304 | tf_op jit(solution)/shard_map/all_to_all | solution.py:116
  87.9 115.0 %all-gather.5.cloned.1.call-start = ((), (), s32[]{:S(2)}) async-start(), calls=%async_computation.7 | async-start | bytes 18874368 | tf_op jit(solution)/shard_map/all_gather | solution.py:168
  119.0 0.9 copy-start.5
  119.9 1.5 copy-start.9
  119.9 1.4 copy-start.2
  121.3 230.9 %reduce-scatter.2.cloned.1.call-start = ((), (), s32[]{:S(2)}) async-start(), calls=%async_computation.8 | async-start | bytes 7077888 | tf_op jit(solution)/shard_map/reduce_scatter | solution.py:193
  123.1 87.4 %copy-start.7 = (f32[4096]{0:T(1024)S(1)}, f32[4096]{0:T(1024)}, u32[]{:S(2)}) copy-start(f32[4096]{0:T(1024)} %param.25) | copy-start | bytes 49156
  212.3 88.3 %slice-start = ((s8[6291456]{0:T(1024)(128)(4,1)}), s8[4194304]{0:T(1024)(128)(4,1)S(1)}, s32[]{:S(2)}) async-start(s8[6291456]{0:T(1024)(128)(4,1)} %bitcast.160), calls=%async_computation.9 | async-start | bytes 8388608
  293.1 7.5 %slice-start.1 = ((s8[6291456]{0:T(1024)(128)(4,1)}), s8[2097152]{0:T(1024)(128)(4,1)S(1)}, s32[]{:S(2)}) async-start(s8[6291456]{0:T(1024)(128)(4,1)} %bitcast.160), calls=%async_computation.10 | async-start | bytes 4194304
  293.1 12.8 %slice-start.2 = ((s8[6291456]{0:T(1024)(128)(4,1)}), s8[4194304]{0:T(1024)(128)(4,1)S(1)}, s32[]{:S(2)}) async-start(s8[6291456]{0:T(1024)(128)(4,1)} %bitcast.162), calls=%async_computation.11 | async-start | bytes 8388608
  300.6 5.3 %slice-start.3 = ((s8[6291456]{0:T(1024)(128)(4,1)}), s8[2097152]{0:T(1024)(128)(4,1)S(1)}, s32[]{:S(2)}) async-start(s8[6291456]{0:T(1024)(128)(4,1)} %bitcast.162), calls=%async_computation.12 | async-start | bytes 4194304
  312.9 48.8 %copy-start.11 = (f32[128,2]{0,1:T(2,128)S(1)}, f32[128,2]{0,1:T(2,128)}, u32[]{:S(2)}) copy-start(f32[128,2]{0,1:T(2,128)} %param.27) | copy-start | bytes 3076
  354.7 30.5 %all-to-all-start.4 = ((f32[16,48,512]{2,1,0:T(8,128)}), f32[16,48,512]{2,1,0:T(8,128)}, u32[]{:S(2)}, u32[]{:S(2)}) async-start(f32[16,48,512]{2,1,0:T(8,128)} %convert_element_type.63), calls=%async_computation.5 | async-start | bytes 3145728 | tf_op jit(solution)/shard_map/all_to_all | solution.py:196
  361.7 42.8 %copy-start.10 = (f32[512]{0:T(512)S(1)}, f32[512]{0:T(512)}, u32[]{:S(2)}) copy-start(f32[512]{0:T(512)} %param.31) | copy-start | bytes 6148
  361.7 43.6 %copy-start.1 = (bf16[128,16,128]{2,1,0:T(8,128)(2,1)S(1)}, bf16[128,16,128]{2,1,0:T(8,128)(2,1)}, u32[]{:S(2)}) copy-start(bf16[128,16,128]{2,1,0:T(8,128)(2,1)} %param.21) | copy-start | bytes 1572868
Sparse Core Ops, SparseCore 0:
  9.5 45.3 all-gather.2
  121.4 81.3 all-gather.4
  313.0 39.1 reduce-scatter.1
